TPU v7x, 512 devices: a whole 4x8x8 slice. The times are simulated.
512 devices in a mesh: section: 8 (over y_lo, core), expert: 32 (over x, z), dp: 2 (over y_hi).
Axes of the slice: x: 4, y: 8 (y_hi: 2, y_lo: 4; y = y_hi * 4 + y_lo), z: 8, core: 2. Of those that a mesh axis runs over, the one named last changes fastest.
Arguments:
- tokens: bfloat16 [1024, 3072], P(('expert', 'dp')), may hold values from -6 to 6
- grad_out: bfloat16 [1024, 3072], P(('expert', 'dp')), may hold values from -6 to 6
- expert_ids: int32 [1024, 2], P(('expert', 'dp')), may hold values from 0 to 3, as said below
- gate_probs: float32 [1024, 2], P(('expert', 'dp')), may hold values from 0.1 to 0.9
- gate_weight: bfloat16 [3072, 32768], P('dp', ('expert', 'section')), may hold values from -0.109375 to 0.109375
- up_weight: bfloat16 [3072, 32768], P('dp', ('expert', 'section')), may hold values from -0.109375 to 0.109375
- down_weight: bfloat16 [3072, 32768], P('dp', ('expert', 'section')), may hold values from -0.0625 to 0.0625
Outputs:
- moe_out: bfloat16 [1024, 3072], P(('expert', 'dp'), 'section')
- grad_tokens: bfloat16 [1024, 3072], P(('expert', 'dp'), 'section')
- grad_gate: bfloat16 [3072, 32768], P('dp', ('expert', 'section'))
- grad_up: bfloat16 [3072, 32768], P('dp', ('expert', 'section'))
- grad_down: bfloat16 [3072, 32768], P('dp', ('expert', 'section'))
Inputs may be any that keep to these rules, and one draw needn't show every extreme that they name: `expert_ids`: each token names two different experts. Among the 16 tokens of one index of expert and dp (aligned blocks of 16 rows) no expert is named more than 12 times. For each index of dp one expert, drawn from the seed, is named exactly 12 times in every block of that index; block b has dp index b % 2.
All inputs are finite; a program needn't handle non-finite values.
Results may differ from a plain program's by a relative error of at most 0.015.
Values may be sent and summed in bfloat16 or wider, within the bound.
A program may use at most 64 MiB of HBM per device.

v0:
```python
import jax
import jax.numpy as jnp
from jax import lax
from jax.sharding import PartitionSpec as P

EXP = 4
CAP = 12


def slot_tables(id_match, gates, capacity):
    chosen = jnp.any(id_match, axis=2)
    gate_share = jnp.sum(jnp.where(id_match, gates, 0.0), axis=2)
    slot_rank = jnp.cumsum(chosen.astype(jnp.int32), axis=1) - 1
    slot_index = jnp.arange(capacity, dtype=jnp.int32)
    pick_table = jnp.logical_and(
        chosen[:, None, :], slot_rank[:, None, :] == slot_index[None, :, None]
    )
    return (pick_table.astype(jnp.float32), gate_share)


def contract_rows(left, right):
    return lax.dot_general(
        left, right, (((0,), (0,)), ((), ())), preferred_element_type=jnp.float32
    )


def contract_cols(left, right):
    return lax.dot_general(
        left, right, (((1,), (1,)), ((), ())), preferred_element_type=jnp.float32
    )


def local(tokens, grad_out, expert_ids, gate_probs, gate_weight, up_weight, down_weight):
    expert_devices = lax.axis_size("expert")
    tok_count, model_width = tokens.shape
    capacity = CAP
    group_size = expert_devices // EXP
    my_expert = lax.axis_index("expert") // group_size
    gate_full, up_full, down_full = (
        lax.all_gather(gate_weight, "dp", axis=0, tiled=True),
        lax.all_gather(up_weight, "dp", axis=0, tiled=True),
        lax.all_gather(down_weight, "dp", axis=0, tiled=True),
    )
    own_match = expert_ids[None, :, :] == jnp.arange(EXP, dtype=jnp.int32)[:, None, None]
    own_picks, own_share = slot_tables(own_match, gate_probs[None, :, :], capacity)
    all_tokens, all_grads = (
        lax.all_gather(tokens, "expert", axis=0, tiled=True),
        lax.all_gather(grad_out, "expert", axis=0, tiled=True),
    )
    all_ids, all_gates = (
        lax.all_gather(expert_ids.astype(jnp.float32), "expert", axis=0, tiled=True),
        lax.all_gather(gate_probs, "expert", axis=0, tiled=True),
    )
    all_ids = all_ids.reshape(expert_devices, tok_count, 2)
    all_gates = all_gates.reshape(expert_devices, tok_count, 2)
    src_match = all_ids == my_expert.astype(jnp.float32)
    src_picks, src_share = slot_tables(src_match, all_gates, capacity)
    src_tokens = all_tokens.reshape(expert_devices, tok_count, model_width)
    src_grads = all_grads.reshape(expert_devices, tok_count, model_width)
    src_scaled = (src_share[:, :, None] * src_grads.astype(jnp.float32)).astype(jnp.bfloat16)
    pick_bf = src_picks.astype(jnp.bfloat16)
    recv_tokens = jnp.einsum(
        "pct,ptd->pcd", pick_bf, src_tokens, preferred_element_type=jnp.float32
    ).astype(jnp.bfloat16)
    recv_grads = jnp.einsum(
        "pct,ptd->pcd", pick_bf, src_scaled, preferred_element_type=jnp.float32
    ).astype(jnp.bfloat16)
    slot_tokens = recv_tokens.reshape(-1, model_width)
    slot_grads = recv_grads.reshape(-1, model_width)
    gate_pre = jnp.dot(slot_tokens, gate_full, preferred_element_type=jnp.float32)
    up_pre = jnp.dot(slot_tokens, up_full, preferred_element_type=jnp.float32)
    sigmoid_gate = jax.nn.sigmoid(gate_pre)
    silu_value = gate_pre * sigmoid_gate
    activation = (silu_value * up_pre).astype(jnp.bfloat16)
    partial_out = contract_cols(activation, down_full)
    act_grad = jnp.dot(slot_grads, down_full, preferred_element_type=jnp.float32)
    up_grad = (act_grad * silu_value).astype(jnp.bfloat16)
    gate_grad = (act_grad * up_pre * sigmoid_gate * (1.0 + gate_pre * (1.0 - sigmoid_gate))).astype(
        jnp.bfloat16
    )
    partial_in = contract_cols(gate_grad, gate_full) + contract_cols(up_grad, up_full)
    summed_grads = lax.psum_scatter(
        jnp.concatenate(
            [
                contract_rows(slot_tokens, gate_grad),
                contract_rows(slot_tokens, up_grad),
                contract_rows(slot_grads, activation),
            ],
            axis=1,
        ).astype(jnp.bfloat16),
        "dp",
        scatter_dimension=0,
        tiled=True,
    ).astype(jnp.float32)
    hidden_dev = gate_weight.shape[1]
    grad_gate = summed_grads[:, :hidden_dev].astype(jnp.bfloat16)
    grad_up = summed_grads[:, hidden_dev : 2 * hidden_dev].astype(jnp.bfloat16)
    grad_down = summed_grads[:, 2 * hidden_dev :].astype(jnp.bfloat16)
    weighted_picks = own_picks * own_share[:, None, :]
    back_out, back_in = (
        lax.all_to_all(
            partial_out.reshape(expert_devices, capacity, model_width).astype(jnp.bfloat16),
            "expert",
            split_axis=0,
            concat_axis=0,
            tiled=True,
        ).astype(jnp.float32),
        lax.all_to_all(
            partial_in.reshape(expert_devices, capacity, model_width).astype(jnp.bfloat16),
            "expert",
            split_axis=0,
            concat_axis=0,
            tiled=True,
        ).astype(jnp.float32),
    )
    sum_out = back_out.reshape(EXP, group_size, capacity, model_width).sum(axis=1)
    sum_in = back_in.reshape(EXP, group_size, capacity, model_width).sum(axis=1)
    token_out = jnp.einsum("ect,ecd->td", weighted_picks, sum_out, precision=lax.Precision.HIGHEST)
    token_in = jnp.einsum("ect,ecd->td", own_picks, sum_in, precision=lax.Precision.HIGHEST)
    final_out, final_in = (
        lax.psum_scatter(
            token_out.astype(jnp.bfloat16), "section", scatter_dimension=1, tiled=True
        ).astype(jnp.float32),
        lax.psum_scatter(
            token_in.astype(jnp.bfloat16), "section", scatter_dimension=1, tiled=True
        ).astype(jnp.float32),
    )
    return (
        final_out.astype(jnp.bfloat16),
        final_in.astype(jnp.bfloat16),
        grad_gate,
        grad_up,
        grad_down,
    )


def solution(mesh):
    return jax.shard_map(
        local,
        mesh=mesh,
        in_specs=(
            P(("expert", "dp"), None),
            P(("expert", "dp"), None),
            P(("expert", "dp"), None),
            P(("expert", "dp"), None),
            P("dp", ("expert", "section")),
            P("dp", ("expert", "section")),
            P("dp", ("expert", "section")),
        ),
        out_specs=(
            P(("expert", "dp"), "section"),
            P(("expert", "dp"), "section"),
            P("dp", ("expert", "section")),
            P("dp", ("expert", "section")),
            P("dp", ("expert", "section")),
        ),
        check_vma=False,
    )
```

profile of v0, /device:TPU:1, one launch (start us, length us, event | category | flops | bytes accessed | tf_op | source)
XLA Modules:
  0.0 403.4 jit_solution(15235942796468195575)
XLA Ops:
  7.2 0.7 all-gather.5.cloned.1.call-update
  7.9 0.7 all-gather.7.cloned.1.call-update
  8.7 0.7 convert_bitcast_fusion
  9.3 40.5 %all-gather = f32[32,16,2]{1,2,0:T(2,128)S(1)} all-gather(f32[1,16,2]{1,2,0:T(2,128)S(1)} %convert_bitcast_fusion), channel_id=1, replica_groups=mesh['section'=8,'expert'=32,'dp'=2] {'expert'}, dimensions={0}, use_global_device_ids=true | all-gather | bytes 4224 | tf_op jit(solution)/shard_map/all_gather | solution.py:51
  50.1 33.7 %all-gather.1 = f32[32,16,2]{1,2,0:T(2,128)S(1)} all-gather(f32[1,16,2]{1,2,0:T(2,128)} %bitcast.51), channel_id=1, replica_groups=mesh['section'=8,'expert'=32,'dp'=2] {'expert'}, dimensions={0}, use_global_device_ids=true | all-gather | bytes 4224 | tf_op jit(solution)/shard_map/all_gather | solution.py:52
  83.8 15.4 %all_gather.23 = bf16[3072,128]{1,0:T(8,128)(2,1)S(1)} all-gather(bf16[1536,128]{1,0:T(8,128)(2,1)} %param.11), channel_id=1, replica_groups=mesh['section'=8,'expert'=32,'dp'=2] {'dp'}, dimensions={0}, use_global_device_ids=true | all-gather | bytes 1179648 | tf_op jit(solution)/shard_map/all_gather | solution.py:40
  99.2 24.8 %all_gather.24 = bf16[3072,128]{1,0:T(8,128)(2,1)} all-gather(bf16[1536,128]{1,0:T(8,128)(2,1)} %param.12), channel_id=1, replica_groups=mesh['section'=8,'expert'=32,'dp'=2] {'dp'}, dimensions={0}, use_global_device_ids=true | all-gather | bytes 1179648 | tf_op jit(solution)/shard_map/all_gather | solution.py:41
  124.0 21.9 %all_gather.25 = bf16[3072,128]{1,0:T(8,128)(2,1)} all-gather(bf16[1536,128]{1,0:T(8,128)(2,1)} %param.13), channel_id=1, replica_groups=mesh['section'=8,'expert'=32,'dp'=2] {'dp'}, dimensions={0}, use_global_device_ids=true | all-gather | bytes 1179648 | tf_op jit(solution)/shard_map/all_gather | solution.py:42
  145.9 4.6 %convolution_convert_fusion.1 = bf16[32,12,3072]{2,1,0:T(8,128)(2,1)} fusion(bf16[32,16,3072]{2,1,0:T(8,128)(2,1)} %bitcast.47, s32[32,16]{1,0:T(8,128)S(1)} %broadcast_add_fusion, pred[32,16]{1,0:T(8,128)(4,1)S(1)} %fusion.22), kind=kOutput, calls=%fused_computation.6 | convolution fusion | flops 38952960 | bytes 5507584 | tf_op jit(solution)/shard_map/pct,ptd->pcd/dot_general | solution.py:62
  150.4 2.8 reshape.71
  153.3 30.1 %all-gather.7.cloned.1.call-done = bf16[512,3072]{1,0:T(8,128)(2,1)} async-done(((bf16[16,3072]{1,0:T(8,128)(2,1)}), bf16[512,3072]{1,0:T(8,128)(2,1)}) %all-gather.7.cloned.1.call-update) | async-done | bytes 3145744 | tf_op jit(solution)/shard_map/all_gather | solution.py:48
  183.3 4.6 %convolution_convert_fusion = bf16[32,12,3072]{2,1,0:T(8,128)(2,1)} fusion(bf16[32,16,3072]{2,1,0:T(8,128)(2,1)} %bitcast.48, f32[32,16]{1,0:T(8,128)S(1)} %select_reduce_fusion, s32[32,16]{1,0:T(8,128)S(1)} %broadcast_add_fusion, pred[32,16]{1,0:T(8,128)(4,1)S(1)} %fusion.22), kind=kOutput, calls=%fused_computation.5 | convolution fusion | flops 43671552 | bytes 5509632 | tf_op jit(solution)/shard_map/pct,ptd->pcd/dot_general | solution.py:65
  188.0 4.3 %reshape.74 = bf16[384,3072]{1,0:T(8,128)(2,1)} reshape(bf16[32,12,3072]{2,1,0:T(8,128)(2,1)} %convolution_convert_fusion) | data formatting | bytes 4718592 | tf_op jit(solution)/shard_map/reshape | solution.py:69
  192.2 0.8 fusion.25
  193.0 0.4 copy-done.1
  193.4 0.8 fusion.26
  194.2 0.9 copy-done
  195.0 0.2 copy-done.3
  195.2 0.8 multiply_convert_fusion
  196.0 2.2 convolution_convert_fusion.2
  198.2 4.2 %convert_element_type.89 = bf16[32,12,3072]{2,1,0:T(8,128)(2,1)} reshape(bf16[384,3072]{1,0:T(8,128)(2,1)} %convolution_convert_fusion.2) | data formatting | bytes 4718592 | tf_op jit(solution)/shard_map/convert_element_type | solution.py:102
  202.5 6.0 %all-to-all-start = ((bf16[32,12,3072]{2,1,0:T(8,128)(2,1)}), bf16[32,12,3072]{2,1,0:T(8,128)(2,1)}, u32[]{:S(2)}, u32[]{:S(2)}) async-start(bf16[32,12,3072]{2,1,0:T(8,128)(2,1)} %convert_element_type.89), calls=%async_computation | async-start | bytes 6291456 | tf_op jit(solution)/shard_map/all_to_all | solution.py:101
  208.6 2.3 convolution_convert_fusion.3
  210.8 0.6 convolution_convert_fusion.4
  211.5 0.6 convolution_convert_fusion.5
  212.1 1.6 pad_maximum_fusion
  213.7 0.8 fusion.27
  214.5 0.3 copy-done.2
  214.8 0.8 add_convert_fusion
  215.6 2.4 convert_element_type.98
  218.0 60.0 %all-to-all-done = bf16[32,12,3072]{2,1,0:T(8,128)(2,1)} async-done(((bf16[32,12,3072]{2,1,0:T(8,128)(2,1)}), bf16[32,12,3072]{2,1,0:T(8,128)(2,1)}, u32[]{:S(2)}, u32[]{:S(2)}) %all-to-all-start) | async-done | bytes 2359328 | tf_op jit(solution)/shard_map/all_to_all | solution.py:101
  278.1 7.3 %all-to-all-start.1 = ((bf16[32,12,3072]{2,1,0:T(8,128)(2,1)}), bf16[32,12,3072]{2,1,0:T(8,128)(2,1)S(1)}, u32[]{:S(2)}, u32[]{:S(2)}) async-start(bf16[32,12,3072]{2,1,0:T(8,128)(2,1)} %convert_element_type.98), calls=%async_computation.1 | async-start | bytes 6291456 | tf_op jit(solution)/shard_map/all_to_all | solution.py:108
  285.4 0.2 reduce-scatter.10.cloned.1.call-start
  285.7 0.2 reduce_window_sum.22
  285.9 2.5 convert_reduce_fusion.1
  288.4 1.0 fusion.1
  289.5 1.2 copy.30
  290.7 65.2 %all-to-all-done.1 = bf16[32,12,3072]{2,1,0:T(8,128)(2,1)S(1)} async-done(((bf16[32,12,3072]{2,1,0:T(8,128)(2,1)}), bf16[32,12,3072]{2,1,0:T(8,128)(2,1)S(1)}, u32[]{:S(2)}, u32[]{:S(2)}) %all-to-all-start.1) | async-done | bytes 2359328 | tf_op jit(solution)/shard_map/all_to_all | solution.py:108
  355.9 0.5 convert_reduce_fusion
  356.5 0.6 fusion.2
  357.1 1.2 copy.32
  358.3 1.3 fusion.24
  359.6 0.9 copy.29
  360.5 0.9 copy.28
  361.5 0.9 copy.27
  362.4 1.6 copy.31
  363.9 31.3 %reduce-scatter.12.cloned.1.call-done = bf16[384,16]{1,0:T(8,128)(2,1)} async-done(((bf16[3072,16]{1,0:T(8,128)(2,1)}), bf16[384,16]{1,0:T(8,128)(2,1)}) %reduce-scatter.12.cloned.1.call-update) | async-done | bytes 12304
  395.3 1.6 copy.33
  (27 shorter events, 0.6 us)
Async XLA Ops:
  7.2 138.7 %all-gather.5.cloned.1.call-start = ((), (), s32[]{:S(2)}) async-start(), calls=%async_computation.5 | async-start | bytes 3244032 | tf_op jit(solution)/shard_map/all_gather | solution.py:47
  7.9 175.4 %all-gather.7.cloned.1.call-start = ((), (), s32[]{:S(2)}) async-start(), calls=%async_computation.6 | async-start | bytes 3244032 | tf_op jit(solution)/shard_map/all_gather | solution.py:48
  192.2 1.1 copy-start.1
  193.4 1.7 copy-start
  193.4 1.8 copy-start.3
  202.5 75.6 %all-to-all-start = ((bf16[32,12,3072]{2,1,0:T(8,128)(2,1)}), bf16[32,12,3072]{2,1,0:T(8,128)(2,1)}, u32[]{:S(2)}, u32[]{:S(2)}) async-start(bf16[32,12,3072]{2,1,0:T(8,128)(2,1)} %convert_element_type.89), calls=%async_computation | async-start | bytes 6291456 | tf_op jit(solution)/shard_map/all_to_all | solution.py:101
  208.5 149.8 %reduce-scatter.8.cloned.1.call-start = ((), (), s32[]{:S(2)}) async-start(), calls=%async_computation.7 | async-start | bytes 3538944 | tf_op jit(solution)/shard_map/reduce_scatter | solution.py:82
  213.7 1.1 copy-start.2
  218.0 67.6 %copy-start.5 = (s32[16,2]{0,1:T(2,128)S(1)}, s32[16,2]{0,1:T(2,128)}, u32[]{:S(2)}) copy-start(s32[16,2]{0,1:T(2,128)} %param.9) | copy-start | bytes 388
  218.0 67.9 %copy-start.4 = (f32[16,2]{0,1:T(2,128)S(1)}, f32[16,2]{0,1:T(2,128)}, u32[]{:S(2)}) copy-start(f32[16,2]{0,1:T(2,128)} %param.10) | copy-start | bytes 388
  278.1 77.9 %all-to-all-start.1 = ((bf16[32,12,3072]{2,1,0:T(8,128)(2,1)}), bf16[32,12,3072]{2,1,0:T(8,128)(2,1)S(1)}, u32[]{:S(2)}, u32[]{:S(2)}) async-start(bf16[32,12,3072]{2,1,0:T(8,128)(2,1)} %convert_element_type.98), calls=%async_computation.1 | async-start | bytes 6291456 | tf_op jit(solution)/shard_map/all_to_all | solution.py:108
  285.4 77.0 %reduce-scatter.10.cloned.1.call-start = ((), (), s32[]{:S(2)}) async-start(), calls=%async_computation.8 | async-start | bytes 884736
  290.7 104.6 %reduce-scatter.12.cloned.1.call-start = ((), (), s32[]{:S(2)}) async-start(), calls=%async_computation.9 | async-start | bytes 884736
Sparse Core Ops, SparseCore 0:
  11.1 86.9 all-gather.4
  101.3 81.9 all-gather.6
  213.8 68.0 reduce-scatter.7
  290.8 41.1 reduce-scatter.9
  358.4 36.8 reduce-scatter.11
where the time goes:
time: 406 us; the launch traced here: 403 us
  waiting for transfers between devices  188 us (46%)
  blocking collectives  136 us (33%)
  local copies, waits for them, and re-layouts  25 us (6%)
  matrix products  20.4 us (5%)
  between operations  13.9 us (3%)
  starting transfers between devices  13.8 us (3%)
  other arithmetic  5.84 us (1%)
    all_to_all x1, waiting for transfers between devices, local(): lax.all_to_all(partial_in.reshape(expert_devices, capacity, model_width)....  65.2 us
    all_to_all x1, waiting for transfers between devices, local(): lax.all_to_all(partial_out.reshape(expert_devices, capacity, model_width)...  60 us
    all_gather x1, blocking collectives, local(): lax.all_gather(expert_ids.astype(jnp.float32), 'expert', axis=0, tiled=True)  40.5 us
    all_gather x1, blocking collectives, local(): lax.all_gather(gate_probs, 'expert', axis=0, tiled=True)  33.7 us
    unnamed x7, waiting for transfers between devices  32.8 us
    all_gather x1, waiting for transfers between devices, local(): lax.all_gather(grad_out, 'expert', axis=0, tiled=True)  30.1 us
    all_gather x1, blocking collectives, local(): lax.all_gather(up_weight, 'dp', axis=0, tiled=True)  24.8 us
    all_gather x1, blocking collectives, local(): lax.all_gather(down_weight, 'dp', axis=0, tiled=True)  21.9 us
  transfers between devices with their start and end apart: 7, of which 4 were waited for; matrix products, arithmetic and copies ran while one was open for 8% of the time, Pallas kernels for 0%

commit v1 on v0

v1 whole, which is shorter than its diff:
```python
import functools

import jax
import jax.numpy as jnp
from jax import lax
from jax.experimental import pallas as pl
from jax.experimental.pallas import tpu as pltpu
from jax.sharding import PartitionSpec as P

EXP = 4
CAP = 12
MESH = pl.DeviceIdType.MESH
F32 = jnp.float32
BF16 = jnp.bfloat16


def rows_dot(left, right):
    return lax.dot_general(left, right, (((0,), (0,)), ((), ())), preferred_element_type=F32)


def cols_dot(left, right):
    return lax.dot_general(left, right, (((1,), (1,)), ((), ())), preferred_element_type=F32)


class Ids:
    def __init__(self, nz, nx, nyl):
        self.count = 0
        half = nz // 2
        self.pair, self.share = self.take(1), self.take(1)
        self.to_expert = self.take(nx)
        self.up, self.down = self.take(half + 1), self.take(half + 1)
        self.twin = self.take(nz)
        self.hop_up, self.hop_down = self.take(nz), self.take(nz)
        self.end_up, self.end_down = self.take(nz), self.take(nz)
        self.out_twin = self.take(nz)
        self.sum_up, self.sum_down = self.take(half + 1), self.take(half + 1)
        self.to_source = self.take(nx)
        self.last = self.take(max(2 * (nyl // 2), nyl))

    def take(self, number):
        first = self.count
        self.count += number
        return first


def kernel(
    dims,
    tok, grd, expert_ids, gate_probs, w_gate, w_up, w_down,
    moe, gin, d_gate, d_up, d_down,
    staged, xs, share, rsend, gathered, weights,
    h_own, h_send, h_relay, h_other, hidden,
    o_own, o_send, o_twin, up_send, down_send, up_recv, down_recv,
    back_send, back_recv, last_send, last_recv, send_sem, recv_sem,
):
    nx, nz, nyl, feats, hid, td = dims
    half, nq = nz // 2, nyl // 2
    ny = 2 * nyl
    xh = nx // 2
    ids = Ids(nz, nx, nyl)
    section, place, yh = lax.axis_index("section"), lax.axis_index("expert"), lax.axis_index("dp")
    x, z = place // nz, lax.rem(place, nz)
    yl, c = section // 2, lax.rem(section, 2)
    y = yh * nyl + yl

    def at(x_to, z_to, y_to, c_to):
        return (lax.rem(y_to, nyl) * 2 + c_to, x_to * nz + z_to, y_to // nyl)

    def ring(value, size):
        return lax.rem(value + 2 * size, size)

    def copy(number, src, dst, to):
        return pltpu.make_async_remote_copy(
            src_ref=src, dst_ref=dst, send_sem=send_sem.at[number], recv_sem=recv_sem.at[number],
            device_id=to, device_id_type=MESH,
        )

    twin = at(x, z, y, 1 - c)
    above, below = at(x, ring(z + 1, nz), y, c), at(x, ring(z - 1, nz), y, c)
    hop = ny // 4
    north, south = at(x, z, ring(y + hop, ny), c), at(x, z, ring(y - hop, ny), c)
    pair = at(x, z, (1 - yh) * nyl + (nyl - 1 - yl), c)

    started = []

    def go(number, src, dst, to):
        one = copy(number, src, dst, to)
        one.start()
        started.append(one)

    def arrived(number, dst):
        copy(number, dst, dst, twin).wait_recv()

    barrier = pltpu.get_barrier_semaphore()
    for step in range(1, 2 * ny):
        other = ring(y * 2 + c + step, 2 * ny)
        pl.semaphore_signal(barrier, inc=1, device_id=at(x, z, other // 2, lax.rem(other, 2)), device_id_type=MESH)
    for step in range(1, nx):
        pl.semaphore_signal(barrier, inc=1, device_id=at(ring(x + step, nx), z, y, c), device_id_type=MESH)
    pl.semaphore_signal(barrier, inc=1, device_id=above, device_id_type=MESH)
    pl.semaphore_signal(barrier, inc=1, device_id=below, device_id_type=MESH)

    lane = lax.broadcasted_iota(jnp.int32, (td, 128), 1)
    gates = jnp.zeros((td, 128), F32)
    for k in range(2):
        gates = gates + jnp.where(expert_ids[:, k : k + 1] == lane, gate_probs[:, k : k + 1], 0.0)
    share[yh] = gates
    other_half = pl.ds(pl.multiple_of((1 - yh) * 2 * feats + c * feats, 128), feats)
    own_half = pl.ds(pl.multiple_of(yh * 2 * feats + c * feats, 128), feats)
    staged[0] = tok[:, other_half]
    staged[1] = grd[:, other_half]
    xs[yh, 0] = tok[:, own_half]
    xs[yh, 1] = grd[:, own_half]
    pl.semaphore_wait(barrier, 2 * ny - 1 + nx - 1 + 2)
    go(ids.pair, staged, xs.at[yh], pair)
    go(ids.share, share.at[yh], share.at[yh], pair)

    for h in range(2):
        part = slice(h * feats, (h + 1) * feats)
        weights[h, :, :hid] = w_gate[part, :]
        weights[h, :, hid : 2 * hid] = w_up[part, :]
        weights[h, :, 2 * hid :] = w_down[part, :]

    arrived(ids.share, share.at[1 - yh])
    arrived(ids.pair, xs.at[1 - yh])

    before = lax.broadcasted_iota(jnp.int32, (td, td), 1) < lax.broadcasted_iota(jnp.int32, (td, td), 0)
    before = jnp.where(before, 1.0, 0.0).astype(BF16)
    chosen = [jnp.where(share[d] > 0.0, 1.0, 0.0) for d in range(2)]
    rank = [jnp.dot(before, chosen[d].astype(BF16), preferred_element_type=F32) for d in range(2)]
    chosen4 = jnp.concatenate(chosen * 2, axis=0)
    rank4 = jnp.concatenate(
        [rank[0], rank[1] + CAP, rank[0] + 2 * CAP, rank[1] + 3 * CAP], axis=0
    )
    slot = lax.broadcasted_iota(jnp.int32, (4 * td, 4 * CAP), 1).astype(F32)

    def picks(e):
        same = jnp.where(rank4[:, e : e + 1] == slot, 1.0, 0.0)
        return (same * chosen4[:, e : e + 1]).astype(BF16)

    for e in range(nx):
        rows = [xs[0, 0], xs[1, 0]]
        for d in range(2):
            rows.append((share[d][:, e : e + 1] * xs[d, 1].astype(F32)).astype(BF16))
        rsend[e] = rows_dot(picks(e), jnp.concatenate(rows, axis=0)).astype(BF16)
    for step in range(1, nx):
        to = ring(x + step, nx)
        go(ids.to_expert + step, rsend.at[to], gathered.at[c, z, x], at(to, z, y, c))
    gathered[c, z, x] = rsend[x]
    for step in range(1, nx):
        arrived(ids.to_expert + step, gathered.at[c, z, ring(x - step, nx)])

    def gather_step(k):
        up_block, down_block = ring(z - k + 1, nz), ring(z + k - 1, nz)
        if k < half:
            up_part, down_part = gathered.at[c, up_block], gathered.at[c, down_block]
        else:
            up_part = gathered.at[c, up_block, pl.ds(0, xh)]
            down_part = gathered.at[c, down_block, pl.ds(xh, xh)]
        go(ids.up + k, up_part, up_part, above)
        go(ids.down + k, down_part, down_part, below)

    def gather_wait(k):
        up_block, down_block = ring(z - k, nz), ring(z + k, nz)
        if k < half:
            up_part, down_part = gathered.at[c, up_block], gathered.at[c, down_block]
        else:
            up_part = gathered.at[c, up_block, pl.ds(0, xh)]
            down_part = gathered.at[c, down_block, pl.ds(xh, xh)]
        arrived(ids.up + k, up_part)
        arrived(ids.down + k, down_part)

    def blocks(k):
        if k == 0:
            return [(z, 0)]
        if k == half:
            return [(ring(z + half, nz), nz - 1)]
        return [(ring(z - k, nz), 2 * k - 1), (ring(z + k, nz), 2 * k)]

    def each(k, body):
        if len(blocks(k)) == 1:
            body(*blocks(k)[0])
        else:
            def turn(i, carry):
                body(ring(z - k + 2 * k * i, nz), 2 * k - 1 + i)
                return carry
            lax.fori_loop(0, 2, turn, 0)

    def twin_share(k):
        for block, number in blocks(k):
            go(ids.twin + number, gathered.at[c, block], gathered.at[c, block], twin)

    slots = 4 * CAP

    def h_compute(k):
        def body(block, number):
            arrived(ids.twin + number, gathered.at[1 - c, block])
            total = jnp.dot(
                gathered[0, block].reshape(nx * slots, feats), weights[0], preferred_element_type=F32
            ) + jnp.dot(
                gathered[1, block].reshape(nx * slots, feats), weights[1], preferred_element_type=F32
            )
            total = total.reshape(nx, slots, 3 * hid)
            value = jnp.concatenate(
                [total[:, : slots // 2, : 2 * hid], total[:, slots // 2 :, 2 * hid :]], axis=2
            ).reshape(nx * slots // 2, 3 * hid)
            h_own[block] = value
            h_send[block] = value.reshape(2, nx * slots // 4, 3 * hid).astype(BF16)
        each(k, body)
        for block, number in blocks(k):
            go(ids.hop_up + number, h_send.at[block, 0], h_relay.at[block, 0], north)
            go(ids.hop_down + number, h_send.at[block, 1], h_relay.at[block, 1], south)

    def relay(k):
        for block, number in blocks(k):
            arrived(ids.hop_up + number, h_relay.at[block, 0])
            go(ids.end_up + number, h_relay.at[block, 0], h_other.at[block, 0], north)
            arrived(ids.hop_down + number, h_relay.at[block, 1])
            go(ids.end_down + number, h_relay.at[block, 1], h_other.at[block, 1], south)

    def outputs(k):
        def body(block, number):
            arrived(ids.end_up + number, h_other.at[block, 0])
            arrived(ids.end_down + number, h_other.at[block, 1])
            full = h_own[block] + h_other[block].reshape(nx * slots // 2, 3 * hid).astype(F32)
            gate_pre, up_pre, act_grad = full[:, :hid], full[:, hid : 2 * hid], full[:, 2 * hid :]
            sigmoid_gate = jax.nn.sigmoid(gate_pre)
            silu = gate_pre * sigmoid_gate
            activation = silu * up_pre
            up_grad = act_grad * silu
            gate_grad = act_grad * up_pre * sigmoid_gate * (1.0 + gate_pre * (1.0 - sigmoid_gate))
            zero = jnp.zeros_like(activation)
            first = jnp.concatenate([gate_grad, up_grad, zero], axis=1).reshape(nx, slots // 2, 3 * hid)
            second = jnp.concatenate([zero, zero, activation], axis=1).reshape(nx, slots // 2, 3 * hid)
            value = jnp.concatenate([first, second], axis=1).reshape(nx * slots, 3 * hid).astype(BF16)
            hidden[block] = value
            o_own[block] = cols_dot(value, weights[c]).reshape(nx, slots, feats)
            o_send[block] = cols_dot(value, weights[1 - c]).reshape(nx, slots, feats).astype(BF16)
        each(k, body)
        for block, number in blocks(k):
            go(ids.out_twin + number, o_send.at[block], o_twin.at[block], twin)

    gather_step(1)
    twin_share(0)
    for k in range(1, half + 1):
        gather_wait(k)
        if k < half:
            gather_step(k + 1)
        twin_share(k)
        h_compute(k - 1)
        if k >= 2:
            relay(k - 2)
        if k >= 3:
            outputs(k - 3)
    h_compute(half)
    relay(half - 1)
    outputs(half - 2)
    relay(half)
    outputs(half - 1)
    outputs(half)

    tile = min(feats, 256)
    tiles = 2 * (feats // tile)

    def weight_grads(first, last):
        def turn(t, carry):
            h, j = t // (feats // tile), lax.rem(t, feats // tile)
            left = gathered[h, :, :, :, pl.ds(pl.multiple_of(j * tile, 128), tile)]
            value = rows_dot(
                left.reshape(nz * nx * slots, tile), hidden[...].reshape(nz * nx * slots, 3 * hid)
            ).astype(BF16)
            rows = pl.ds(pl.multiple_of(t * tile, 128), tile)
            d_gate[rows, :] = value[:, :hid]
            d_up[rows, :] = value[:, hid : 2 * hid]
            d_down[rows, :] = value[:, 2 * hid :]
            return carry
        lax.fori_loop(first, last, turn, 0)

    def own_sum(block):
        return o_own[block] + o_twin[block].astype(F32)

    def out_arrived(k):
        for block, number in blocks(k):
            arrived(ids.out_twin + number, o_twin.at[block])

    out_arrived(half)
    far = ring(z + half, nz)
    value = own_sum(far).astype(BF16)
    up_send[1, :xh] = value[:xh]
    down_send[1, xh:] = value[xh:]
    go(ids.sum_up + 1, up_send.at[1, pl.ds(0, xh)], up_recv.at[1, pl.ds(0, xh)], above)
    go(ids.sum_down + 1, down_send.at[1, pl.ds(xh, xh)], down_recv.at[1, pl.ds(xh, xh)], below)
    done = 0
    for step in range(2, half + 1):
        until = (tiles * (step - 1)) // (half - 1)
        weight_grads(done, until)
        done = until
        away = half + 1 - step
        out_arrived(away)
        if step == 2:
            up_send[step] = own_sum(ring(z + away, nz)).astype(BF16)
            down_send[step] = own_sum(ring(z - away, nz)).astype(BF16)
            arrived(ids.sum_up + 1, up_recv.at[1, pl.ds(0, xh)])
            part = own_sum(ring(z + away, nz))[:xh] + up_recv[1, :xh].astype(F32)
            up_send[step, :xh] = part.astype(BF16)
            go(ids.sum_up + step, up_send.at[step], up_recv.at[step], above)
            arrived(ids.sum_down + 1, down_recv.at[1, pl.ds(xh, xh)])
            part = own_sum(ring(z - away, nz))[xh:] + down_recv[1, xh:].astype(F32)
            down_send[step, xh:] = part.astype(BF16)
            go(ids.sum_down + step, down_send.at[step], down_recv.at[step], below)
        else:
            arrived(ids.sum_up + step - 1, up_recv.at[step - 1])
            value = own_sum(ring(z + away, nz)) + up_recv[step - 1].astype(F32)
            up_send[step] = value.astype(BF16)
            go(ids.sum_up + step, up_send.at[step], up_recv.at[step], above)
            arrived(ids.sum_down + step - 1, down_recv.at[step - 1])
            value = own_sum(ring(z - away, nz)) + down_recv[step - 1].astype(F32)
            down_send[step] = value.astype(BF16)
            go(ids.sum_down + step, down_send.at[step], down_recv.at[step], below)
    out_arrived(0)
    arrived(ids.sum_up + half, up_recv.at[half])
    arrived(ids.sum_down + half, down_recv.at[half])
    value = own_sum(z) + up_recv[half].astype(F32) + down_recv[half].astype(F32)
    back_send[...] = value.astype(BF16)
    for step in range(1, nx):
        to = ring(x + step, nx)
        go(ids.to_source + step, back_send.at[to], back_recv.at[x], at(to, z, y, c))
    back_recv[x] = back_send[x]
    for step in range(1, nx):
        source = ring(x - step, nx)
        arrived(ids.to_source + step, back_recv.at[source])

    combined = jnp.zeros((4 * td, feats), F32)
    ones = jnp.ones((td, 1), F32)
    for e in range(nx):
        scale = jnp.concatenate([ones, ones, share[0][:, e : e + 1], share[1][:, e : e + 1]], axis=0)
        picked = jnp.dot(picks(e), back_recv[e], preferred_element_type=F32)
        combined = combined + scale * picked
    combined = combined.astype(BF16)
    width = feats // nq
    for d in range(2):
        for q in range(nq):
            columns = slice(q * width, (q + 1) * width)
            last_send[d, q, :td] = combined[d * td : (d + 1) * td, columns]
            last_send[d, q, td:] = combined[(2 + d) * td : (3 + d) * td, columns]
    copies = []
    for d in range(2):
        for q in range(nq):
            owner = yh * nyl + c * nq + q
            y_to, c_to = d * nyl + owner // 2, lax.rem(owner, 2)
            mine = jnp.logical_and(y_to == y, c_to == c)
            one = pltpu.make_async_remote_copy(
                src_ref=last_send.at[d, q], dst_ref=last_recv.at[yl],
                send_sem=send_sem.at[ids.last + d * nq + q], recv_sem=recv_sem.at[ids.last + yl],
                device_id=at(x, z, y_to, c_to), device_id_type=MESH,
            )
            copies.append((mine, one))

            @pl.when(mine)
            def _():
                last_recv[yl] = last_send[d, q]

            @pl.when(jnp.logical_not(mine))
            def _():
                one.start()

    from_yh, from_c = section // nyl, lax.rem(section, nyl) // nq
    for yl_from in range(nyl):
        mine = jnp.logical_and(from_yh * nyl + yl_from == y, from_c == c)

        @pl.when(jnp.logical_not(mine))
        def _():
            arrived(ids.last + yl_from, last_recv.at[yl_from])

    total = last_recv[0].astype(F32)
    for yl_from in range(1, nyl):
        total = total + last_recv[yl_from].astype(F32)
    gin[...] = total[:td].astype(BF16)
    moe[...] = total[td:].astype(BF16)

    for one in started:
        one.wait_send()
    for mine, one in copies:

        @pl.when(jnp.logical_not(mine))
        def _():
            one.wait_send()


def local(nyl, tokens, grad_out, expert_ids, gate_probs, gate_weight, up_weight, down_weight):
    td, width = tokens.shape
    hid = gate_weight.shape[1]
    nx = EXP
    nz = lax.axis_size("expert") // nx
    feats = width // 4
    nq = nyl // 2
    slots = 4 * CAP
    half = nz // 2
    count = Ids(nz, nx, nyl).count
    vmem = pl.BlockSpec(memory_space=pltpu.VMEM)
    out_token = jax.ShapeDtypeStruct((td, width // (2 * nyl)), BF16)
    out_weight = jax.ShapeDtypeStruct(gate_weight.shape, BF16)
    exchange = pltpu.VMEM((nz, 2, nx * slots // 4, 3 * hid), BF16)
    ring_slots = pltpu.VMEM((half + 1, nx, slots, feats), BF16)
    return pl.pallas_call(
        functools.partial(kernel, (nx, nz, nyl, feats, hid, td)),
        out_shape=(out_token, out_token, out_weight, out_weight, out_weight),
        in_specs=[vmem] * 7,
        out_specs=(vmem,) * 5,
        scratch_shapes=[
            pltpu.VMEM((2, td, feats), BF16),
            pltpu.VMEM((2, 2, td, feats), BF16),
            pltpu.VMEM((2, td, 128), F32),
            pltpu.VMEM((nx, slots, feats), BF16),
            pltpu.VMEM((2, nz, nx, slots, feats), BF16),
            pltpu.VMEM((2, feats, 3 * hid), BF16),
            pltpu.VMEM((nz, nx * slots // 2, 3 * hid), F32),
            exchange,
            exchange,
            exchange,
            pltpu.VMEM((nz, nx * slots, 3 * hid), BF16),
            pltpu.VMEM((nz, nx, slots, feats), F32),
            pltpu.VMEM((nz, nx, slots, feats), BF16),
            pltpu.VMEM((nz, nx, slots, feats), BF16),
            ring_slots,
            ring_slots,
            ring_slots,
            ring_slots,
            pltpu.VMEM((nx, slots, feats), BF16),
            pltpu.VMEM((nx, slots, feats), BF16),
            pltpu.VMEM((2, nq, 2 * td, feats // nq), BF16),
            pltpu.VMEM((nyl, 2 * td, feats // nq), BF16),
            pltpu.SemaphoreType.DMA((count,)),
            pltpu.SemaphoreType.DMA((count,)),
        ],
        compiler_params=pltpu.CompilerParams(
            collective_id=0, has_side_effects=True, vmem_limit_bytes=60 * 1024 * 1024
        ),
        name="moe_layer",
    )(tokens, grad_out, expert_ids, gate_probs, gate_weight, up_weight, down_weight)


def solution(mesh):
    return jax.shard_map(
        functools.partial(local, mesh.shape["section"] // 2),
        mesh=mesh,
        in_specs=(
            P(("expert", "dp"), None),
            P(("expert", "dp"), None),
            P(("expert", "dp"), None),
            P(("expert", "dp"), None),
            P("dp", ("expert", "section")),
            P("dp", ("expert", "section")),
            P("dp", ("expert", "section")),
        ),
        out_specs=(
            P(("expert", "dp"), "section"),
            P(("expert", "dp"), "section"),
            P("dp", ("expert", "section")),
            P("dp", ("expert", "section")),
            P("dp", ("expert", "section")),
        ),
        check_vma=False,
    )
```

time: 406 us -> 126 us (0.31)
  waiting for transfers between devices: 188 us -> 0 us
  blocking collectives: 136 us -> 0 us
  Pallas kernels: 0 us -> 117 us
  matrix products: 20.4 us -> 0 us
  local copies, waits for them, and re-layouts: 25 us -> 7.66 us
  starting transfers between devices: 13.8 us -> 0 us
  between operations: 13.9 us -> 0.66 us
  other arithmetic: 5.84 us -> 0 us
    all_gather x5 -> x0, blocking collectives: 136 us -> none  [the longest x1 40.5 us: local(): lax.all_gather(expert_ids.astype(jnp.float32), 'expert', axis=0, tiled=True)]
    all_to_all x2 -> x0, waiting for transfers between devices: 125 us -> none  [the longest x1 65.2 us: local(): lax.all_to_all(partial_in.reshape(expert_devices, capacity, model_width)....]
    pallas_call x0 -> x1, Pallas kernels: none -> 117 us  [local(): pl.pallas_call(functools.partial(kernel, (nx, nz, nyl, feats, hid, td)),...]
    unnamed x7 -> x0, waiting for transfers between devices: 32.8 us -> none
    all_gather x2 -> x0, waiting for transfers between devices: 30.1 us -> none  [the longest x1 30.1 us: local(): lax.all_gather(grad_out, 'expert', axis=0, tiled=True)]
    dot_general x13 -> x0, matrix products: 20.4 us -> none  [the longest x1 4.63 us: local(): jnp.einsum('pct,ptd->pcd', pick_bf, src_scaled, preferred_element_type=jn...]
    all_to_all x2 -> x0, starting transfers between devices: 13.4 us -> none  [the longest x1 7.34 us: local(): lax.all_to_all(partial_in.reshape(expert_devices, capacity, model_width)....]
    reshape x2 -> x0, local copies, waits for them, and re-layouts: 7.1 us -> none  [the longest x1 4.27 us: local(): slot_grads = recv_grads.reshape(-1, model_width)]
  transfers between devices with their start and end apart: 7 -> 0, of which waited for: 4 -> 0; matrix products, arithmetic and copies ran while one was open for 8% -> 0% of each run, Pallas kernels for 0% -> 0%
where the time goes in v1:
time: 126 us
  Pallas kernels  117 us (93%)
  local copies, waits for them, and re-layouts  7.66 us (6%)
    pallas_call x1, Pallas kernels, local(): pl.pallas_call(functools.partial(kernel, (nx, nz, nyl, feats, hid, td)),...  117 us
    unnamed x15, local copies, waits for them, and re-layouts  7.66 us

profile of v1, /device:TPU:1, one launch (start us, length us, event | category | flops | bytes accessed | tf_op | source)
XLA Modules:
  0.0 125.8 jit_solution(654834930968976331)
XLA Ops:
  0.6 0.0 copy-start.3
  0.6 1.4 %copy.12.expert_ids = s32[16,2]{1,0:T(8,128)} copy(s32[16,2]{0,1:T(2,128)} %param.9) | data formatting | bytes 256 | tf_op args[2]
  2.0 0.0 copy-done.3
  2.0 0.7 copy.13.gate_probs
  2.7 117.5 %moe_layer.1 = (bf16[16,384]{1,0:T(8,128)(2,1)}, bf16[16,384]{1,0:T(8,128)(2,1)}, bf16[1536,128]{1,0:T(8,128)(2,1)}, bf16[1536,128]{1,0:T(8,128)(2,1)}, bf16[1536,128]{1,0:T(8,128)(2,1)}) custom-call(bf16[16,3072]{1,0:T(8,128)(2,1)} %tok.1, bf16[16,3072]{1,0:T(8,128)(2,1)} %grd.1, s32[16,2]{1,0:T(8,128)} %copy.12.expert_ids, f32[16,2]{1,0:T(8,128)} %copy.13.gate_probs, ...), custom_call_target="tpu_custom_call" | custom-call | tf_op jit(solution)/shard_map/moe_layer/pallas_call | solution.py:404
  120.1 0.0 copy-start.2
  120.2 1.3 %copy.19 = bf16[16,384]{1,0:T(8,128)(2,1)} copy(bf16[16,384]{1,0:T(8,128)(2,1)} %get-tuple-element.10) | data formatting | bytes 24576
  121.5 0.0 copy-done.2
  121.5 0.6 copy.20
  122.1 0.0 copy-start.1
  122.1 1.8 %copy.21 = bf16[1536,128]{1,0:T(8,128)(2,1)} copy(bf16[1536,128]{1,0:T(8,128)(2,1)} %get-tuple-element.12) | data formatting | bytes 786432
  123.9 0.0 copy-done.1
  123.9 0.0 copy-start
  123.9 0.7 copy.22
  124.6 0.4 copy-done
  125.0 0.7 copy.23
Async XLA Ops:
  0.6 1.4 %copy-start.3 = (f32[16,2]{0,1:T(2,128)S(1)}, f32[16,2]{0,1:T(2,128)}, u32[]{:S(2)}) copy-start(f32[16,2]{0,1:T(2,128)} %param.10) | copy-start | bytes 388
  120.1 1.3 %copy-start.2 = (bf16[16,384]{1,0:T(8,128)(2,1)S(1)}, bf16[16,384]{1,0:T(8,128)(2,1)}, u32[]{:S(2)}) copy-start(bf16[16,384]{1,0:T(8,128)(2,1)} %get-tuple-element.11) | copy-start | bytes 36868
  122.1 1.8 %copy-start.1 = (bf16[1536,128]{1,0:T(8,128)(2,1)S(1)}, bf16[1536,128]{1,0:T(8,128)(2,1)}, u32[]{:S(2)}) copy-start(bf16[1536,128]{1,0:T(8,128)(2,1)} %get-tuple-element.13) | copy-start | bytes 1179652
  123.9 1.1 copy-start

commit v2 on v0

v2 whole, which is shorter than its diff:
```python
import functools

import jax
import jax.numpy as jnp
from jax import lax
from jax.experimental import pallas as pl
from jax.experimental.pallas import tpu as pltpu
from jax.sharding import PartitionSpec as P

EXP = 4
CAP = 12
MESH = pl.DeviceIdType.MESH
F32 = jnp.float32
BF16 = jnp.bfloat16


def rows_dot(left, right):
    return lax.dot_general(left, right, (((0,), (0,)), ((), ())), preferred_element_type=F32)


def cols_dot(left, right):
    return lax.dot_general(left, right, (((1,), (1,)), ((), ())), preferred_element_type=F32)


LAG = 2


def kernel(
    dims,
    tok, grd, expert_ids, gate_probs, w_gate, w_up, w_down,
    moe, gin, d_gate, d_up, d_down,
    staged, xs, share, picks, scales, rsend, gathered, weights,
    h_own, h_send, h_other, hidden,
    o_own, o_send, o_twin, up_send, down_send, up_recv, down_recv,
    back_send, back_recv, last_send, last_recv, grads, send_sem, recv_sem, load_sem,
):
    nx, nz, nyl, feats, hid, td = dims
    half, nq = nz // 2, nyl // 2
    ny = 2 * nyl
    slots = 4 * CAP
    near = slots // 2
    section, place, yh = lax.axis_index("section"), lax.axis_index("expert"), lax.axis_index("dp")
    x, z = place // nz, lax.rem(place, nz)
    yl, c = section // 2, lax.rem(section, 2)
    y = yh * nyl + yl

    def at(x_to, z_to, y_to, c_to):
        return (lax.rem(y_to, nyl) * 2 + c_to, x_to * nz + z_to, y_to // nyl)

    def ring(value, size):
        return lax.rem(value + 2 * size, size)

    twin = at(x, z, y, 1 - c)
    above, below = at(x, ring(z + 1, nz), y, c), at(x, ring(z - 1, nz), y, c)
    across = at(x, z, ring(y + nyl, ny), c)
    pair = at(x, z, (1 - yh) * nyl + (nyl - 1 - yl), c)

    numbers = {}
    started = []

    def number_of(name):
        return numbers.setdefault(name, len(numbers))

    def copy(name, src, dst, to):
        number = number_of(name)
        return pltpu.make_async_remote_copy(
            src_ref=src, dst_ref=dst, send_sem=send_sem.at[number], recv_sem=recv_sem.at[number],
            device_id=to, device_id_type=MESH,
        )

    def go(name, src, dst, to):
        one = copy(name, src, dst, to)
        one.start()
        started.append(one)

    def arrived(name, dst):
        copy(name, dst, dst, twin).wait_recv()

    loads = []
    for h in range(2):
        for i, ref in enumerate((w_gate, w_up, w_down)):
            load = pltpu.make_async_copy(
                ref.at[pl.ds(h * feats, feats), :], weights.at[h, :, pl.ds(i * hid, hid)], load_sem.at[3 * h + i]
            )
            load.start()
            loads.append(load)
    barrier = pltpu.get_barrier_semaphore()
    for step in range(1, 2 * ny):
        other = ring(y * 2 + c + step, 2 * ny)
        pl.semaphore_signal(barrier, inc=1, device_id=at(x, z, other // 2, lax.rem(other, 2)), device_id_type=MESH)
    for step in range(1, nx):
        pl.semaphore_signal(barrier, inc=1, device_id=at(ring(x + step, nx), z, y, c), device_id_type=MESH)
    pl.semaphore_signal(barrier, inc=1, device_id=above, device_id_type=MESH)
    pl.semaphore_signal(barrier, inc=1, device_id=below, device_id_type=MESH)

    row = lax.broadcasted_iota(jnp.int32, (128, td), 0)
    gates = jnp.zeros((128, td), F32)
    for k in range(2):
        gates = gates + jnp.where(expert_ids[k : k + 1, :] == row, gate_probs[k : k + 1, :], 0.0)
    share[yh] = gates.T
    other_half = pl.ds(pl.multiple_of((1 - yh) * 2 * feats + c * feats, 128), feats)
    own_half = pl.ds(pl.multiple_of(yh * 2 * feats + c * feats, 128), feats)
    staged[0] = tok[:, other_half]
    staged[1] = grd[:, other_half]
    xs[yh, 0] = tok[:, own_half]
    xs[yh, 1] = grd[:, own_half]
    pl.semaphore_wait(barrier, 2 * ny - 1 + nx - 1 + 2)
    go("share", share.at[yh], share.at[yh], pair)
    go("pair", staged, xs.at[yh], pair)

    before = lax.broadcasted_iota(jnp.int32, (td, td), 1) < lax.broadcasted_iota(jnp.int32, (td, td), 0)
    before = jnp.where(before, 1.0, 0.0).astype(BF16)
    slot = lax.broadcasted_iota(jnp.int32, (2 * td, slots), 1).astype(F32)
    shift = jnp.where(lax.broadcasted_iota(jnp.int32, (2 * td, 1), 0) < td, 0.0, 2.0 * CAP)

    def tables(d):
        gate = share[d]
        first = (d * CAP).astype(F32)
        chosen = jnp.where(gate > 0.0, 1.0, 0.0)
        rank = jnp.dot(before, chosen.astype(BF16), preferred_element_type=F32)
        ones = jnp.ones((td, 128), F32)
        for e in range(nx):
            rank_e, chosen_e = rank[:, e : e + 1], chosen[:, e : e + 1]
            rank2 = jnp.concatenate([rank_e, rank_e], axis=0) + (shift + first)
            chosen2 = jnp.concatenate([chosen_e, chosen_e], axis=0)
            picks[e, d] = (jnp.where(rank2 == slot, 1.0, 0.0) * chosen2).astype(BF16)
            gate_e = jnp.broadcast_to(gate[:, e : e + 1], (td, 128))
            scales[e, d] = jnp.concatenate([ones, gate_e], axis=0)

    tables(yh)
    arrived("share", share.at[1 - yh])
    tables(1 - yh)
    arrived("pair", xs.at[1 - yh])
    stacked = xs[...].reshape(4 * td, feats).astype(F32)

    def pick_for(e):
        scale = scales[e].reshape(4 * td, 128)[:, :1]
        rows = (scale * stacked).astype(BF16)
        return rows_dot(picks[e].reshape(4 * td, slots), rows).astype(BF16)

    def first_of(k):
        return 0 if k == 0 else 2 * k - 1

    def size_of(k):
        return 1 if k in (0, half) else 2

    def span(k):
        return pl.ds(first_of(k), size_of(k))

    def landing(k, side):
        return nz - 1 if k == half else 2 * k - 1 + side

    def sends(t, k, p, side):
        return k < half or p == side

    width = feats // 2

    def column(i):
        return slice(i * width, (i + 1) * width)

    def columns_of(ref, i):
        return ref.at[:, pl.ds(i * width, width)]

    def gather_send(t, k, p):
        for i in range(2):
            for side, to in ((0, above), (1, below)):
                if sends(t, k, p, side):
                    part = columns_of(gathered.at[c, t, 0, p], i)
                    go(("gather", t, k, p, i, side), part, columns_of(gathered.at[c, t, landing(k, side), p], i), to)

    def gather_take(t, k):
        for p in range(2):
            for i in range(2):
                for side, to in ((0, above), (1, below)):
                    if sends(t, k, p, side):
                        part = columns_of(gathered.at[c, t, landing(k, side), p], i)
                        arrived(("gather", t, k, p, i, side), part)
                        if k < half and sends(t, k + 1, p, side):
                            there = columns_of(gathered.at[c, t, landing(k + 1, side), p], i)
                            go(("gather", t, k + 1, p, i, side), part, there, to)
        twin_share(t, k)

    def twin_share(t, k):
        part = gathered.at[c, t, span(k)]
        go(("twin", t, k), part, part, twin)

    def compute_h(t, k):
        arrived(("twin", t, k), gathered.at[1 - c, t, span(k)])
        n, first = size_of(k), first_of(k)
        total = jnp.dot(
            gathered[0, t, first : first + n].reshape(n * 2 * slots, feats), weights[0], preferred_element_type=F32
        ) + jnp.dot(
            gathered[1, t, first : first + n].reshape(n * 2 * slots, feats), weights[1], preferred_element_type=F32
        )
        total = total.reshape(n * 2, slots, 3 * hid)
        value = jnp.concatenate([total[:, :near, : 2 * hid], total[:, near:, 2 * hid :]], axis=2)
        value = value.reshape(n, slots, 3 * hid)
        h_own[t, first : first + n] = value
        h_send[t, first : first + n] = value.astype(BF16)
        for b in range(first, first + n):
            go(("swap", t, b), h_send.at[t, b], h_other.at[t, b], across)

    def outputs(t, k):
        n, first = size_of(k), first_of(k)
        for b in range(first, first + n):
            arrived(("swap", t, b), h_other.at[t, b])
        full = h_own[t, first : first + n] + h_other[t, first : first + n].astype(F32)
        full = full.reshape(n * slots, 3 * hid)
        gate_pre, up_pre, act_grad = full[:, :hid], full[:, hid : 2 * hid], full[:, 2 * hid :]
        sigmoid_gate = jax.nn.sigmoid(gate_pre)
        silu = gate_pre * sigmoid_gate
        activation = silu * up_pre
        up_grad = act_grad * silu
        gate_grad = act_grad * up_pre * sigmoid_gate * (1.0 + gate_pre * (1.0 - sigmoid_gate))
        zero = jnp.zeros_like(activation)
        upper = jnp.concatenate([gate_grad, up_grad, zero], axis=1).reshape(n * 2, near, 3 * hid)
        lower = jnp.concatenate([zero, zero, activation], axis=1).reshape(n * 2, near, 3 * hid)
        value = jnp.concatenate([upper, lower], axis=1).reshape(n * 2 * slots, 3 * hid).astype(BF16)
        hidden[t, first : first + n] = value.reshape(n, 2, slots, 3 * hid)
        o_send[t, first : first + n] = cols_dot(value, weights[1 - c]).astype(BF16).reshape(n, 2, slots, feats)
        go(("out", t, k), o_send.at[t, span(k)], o_twin.at[t, span(k)], twin)
        o_own[t, first : first + n] = cols_dot(value, weights[c]).reshape(n, 2, slots, feats)

    def own_sum(t, b, p, i):
        return o_own[t, b, p, :, column(i)] + o_twin[t, b, p, :, column(i)].astype(F32)

    def sum_step(t, step):
        away = half + 1 - step
        arrived(("out", t, away), o_twin.at[t, span(away)])
        parts = [(p, i, side) for p in range(2) for i in range(2) for side in range(2)]
        if step == 1:
            parts = [part for part in parts if part[0] == part[2]]
        if step == 2:
            parts.sort(key=lambda part: part[0] == part[2])
        for p, i, side in parts:
            to, out_ref, in_ref = ((above, up_send, up_recv), (below, down_send, down_recv))[side]
            value = own_sum(t, nz - 1 if step == 1 else 2 * away - side, p, i)
            if step > 2 or (step == 2 and p == side):
                arrived(("sum", t, step - 1, p, i, side), columns_of(in_ref.at[t, step - 1, p], i))
                value = value + in_ref[t, step - 1, p, :, column(i)].astype(F32)
            out_ref[t, step, p, :, column(i)] = value.astype(BF16)
            go(
                ("sum", t, step, p, i, side),
                columns_of(out_ref.at[t, step, p], i), columns_of(in_ref.at[t, step, p], i), to,
            )

    def sum_end(t):
        arrived(("out", t, 0), o_twin.at[t, span(0)])
        for p in range(2):
            j = 2 * t + p
            for i in range(2):
                for side, in_ref in ((0, up_recv), (1, down_recv)):
                    arrived(("sum", t, half, p, i, side), columns_of(in_ref.at[t, half, p], i))
                value = own_sum(t, 0, p, i) + up_recv[t, half, p, :, column(i)].astype(F32)
                value = value + down_recv[t, half, p, :, column(i)].astype(F32)
                if j:
                    back_send[t, p, :, column(i)] = value.astype(BF16)
                else:
                    back_recv[0, :, column(i)] = value.astype(BF16)
            if j:
                go(("back", j), back_send.at[t, p], back_recv.at[j], at(ring(x - j, nx), z, y, c))

    def combine(t):
        total = jnp.zeros((4 * td, feats), F32)
        for j in (2 * t, 2 * t + 1):
            if j:
                arrived(("back", j), back_recv.at[j])
            e = ring(x + j, nx)
            scale = scales[e].reshape(4 * td, 128)[:, :1]
            total = total + scale * jnp.dot(
                picks[e].reshape(4 * td, slots), back_recv[j], preferred_element_type=F32
            )
        return total

    tile = min(feats, 256)
    tiles = 2 * (feats // tile)

    def weight_grads(first, last):
        def turn(i, carry):
            h, j = i // (feats // tile), lax.rem(i, feats // tile)
            left = gathered[h, :, :, :, :, pl.ds(pl.multiple_of(j * tile, 128), tile)]
            value = rows_dot(
                left.reshape(nz * nx * slots, tile), hidden[...].reshape(nz * nx * slots, 3 * hid)
            ).astype(BF16)
            rows = pl.ds(pl.multiple_of(i * tile, 128), tile)
            for part in range(3):
                grads[part, rows, :] = value[:, part * hid : (part + 1) * hid]
            return carry
        lax.fori_loop(first, last, turn, 0)

    gathered[c, 0, 0, 0] = pick_for(x)
    gather_send(0, 1, 0)
    for j in range(1, nx):
        e = ring(x + j, nx)
        rsend[j] = pick_for(e)
        go(("expert", j), rsend.at[j], gathered.at[c, j // 2, 0, j % 2], at(e, z, y, c))
    arrived(("expert", 1), gathered.at[c, 0, 0, 1])
    gather_send(0, 1, 1)
    twin_share(0, 0)

    def valid(k):
        return 0 <= k <= half

    for turn in range(1, half + LAG + 1):
        if turn <= half:
            gather_take(0, turn)
        if turn == LAG:
            for p in range(2):
                arrived(("expert", 2 + p), gathered.at[c, 1, 0, p])
                gather_send(1, 1, p)
            twin_share(1, 0)
        if turn == 1:
            for load in loads:
                load.wait()
        if valid(turn - 1):
            compute_h(0, turn - 1)
        if turn > LAG:
            gather_take(1, turn - LAG)
        if valid(turn - LAG - 1):
            compute_h(1, turn - LAG - 1)
        if valid(turn - 3):
            outputs(0, turn - 3)
        if valid(turn - LAG - 3):
            outputs(1, turn - LAG - 3)
    compute_h(1, half)
    for k in range(half + LAG - 2, half + 1):
        outputs(0, k)
    sum_step(0, 1)
    for step in range(2, half):
        outputs(1, half + step - 4)
        sum_step(0, step)
    for k in range(2 * half - 4, half + 1):
        outputs(1, k)
    sum_step(1, 1)
    weight_grads(0, tiles // 6)
    sum_step(0, half)
    weight_grads(tiles // 6, tiles // 3)
    sum_step(1, 2)
    weight_grads(tiles // 3, tiles // 2)
    sum_end(0)
    for step in range(3, half):
        sum_step(1, step)
    weight_grads(tiles // 2, tiles)
    results = []
    for i, ref in enumerate((d_gate, d_up, d_down)):
        result = pltpu.make_async_copy(grads.at[i], ref, load_sem.at[6 + i])
        result.start()
        results.append(result)
    if half > 2:
        sum_step(1, half)
    combined = combine(0)
    sum_end(1)
    combined = (combined + combine(1)).astype(BF16)
    share_of = feats // nq
    for d in range(2):
        for q in range(nq):
            last_send[d, q] = combined[2 * d * td : 2 * (d + 1) * td, q * share_of : (q + 1) * share_of]
    copies = []
    senders = [number_of(("last", i)) for i in range(2 * nq)]
    takers = [number_of(("take", i)) for i in range(nyl)]
    for d in range(2):
        for q in range(nq):
            owner = yh * nyl + c * nq + q
            y_to, c_to = d * nyl + owner // 2, lax.rem(owner, 2)
            mine = jnp.logical_and(y_to == y, c_to == c)
            one = pltpu.make_async_remote_copy(
                src_ref=last_send.at[d, q], dst_ref=last_recv.at[yl],
                send_sem=send_sem.at[senders[d * nq + q]], recv_sem=recv_sem.at[takers[0] + yl],
                device_id=at(x, z, y_to, c_to), device_id_type=MESH,
            )
            copies.append((mine, one))

            @pl.when(mine)
            def _():
                last_recv[yl] = last_send[d, q]

            @pl.when(jnp.logical_not(mine))
            def _():
                one.start()

    from_yh, from_c = section // nyl, lax.rem(section, nyl) // nq
    for yl_from in range(nyl):
        mine = jnp.logical_and(from_yh * nyl + yl_from == y, from_c == c)

        @pl.when(jnp.logical_not(mine))
        def _():
            arrived(("take", yl_from), last_recv.at[yl_from])

    total = last_recv[0].astype(F32)
    for yl_from in range(1, nyl):
        total = total + last_recv[yl_from].astype(F32)
    gin[...] = total[:td].astype(BF16)
    moe[...] = total[td:].astype(BF16)

    for one in results:
        one.wait()
    for one in started:
        one.wait_send()
    for mine, one in copies:

        @pl.when(jnp.logical_not(mine))
        def _():
            one.wait_send()


SEMAPHORES = 192


def local(nyl, tokens, grad_out, expert_ids, gate_probs, gate_weight, up_weight, down_weight):
    td, width = tokens.shape
    hid = gate_weight.shape[1]
    nx = EXP
    nz = lax.axis_size("expert") // nx
    feats = width // 4
    nq = nyl // 2
    slots = 4 * CAP
    half = nz // 2
    vmem = pl.BlockSpec(memory_space=pltpu.VMEM)
    out_token = jax.ShapeDtypeStruct((td, width // (2 * nyl)), BF16)
    out_weight = jax.ShapeDtypeStruct(gate_weight.shape, BF16)
    exchange = pltpu.VMEM((2, nz, slots, 3 * hid), BF16)
    outs = pltpu.VMEM((2, nz, 2, slots, feats), BF16)
    ring_slots = pltpu.VMEM((2, half + 1, 2, slots, feats), BF16)
    anywhere = pl.BlockSpec(memory_space=pl.ANY)
    results = pl.pallas_call(
        functools.partial(kernel, (nx, nz, nyl, feats, hid, td)),
        out_shape=(out_token, out_token, out_weight, out_weight, out_weight),
        in_specs=[vmem] * 4 + [anywhere] * 3,
        out_specs=(vmem,) * 2 + (anywhere,) * 3,
        scratch_shapes=[
            pltpu.VMEM((2, td, feats), BF16),
            pltpu.VMEM((2, 2, td, feats), BF16),
            pltpu.VMEM((2, td, 128), F32),
            pltpu.VMEM((nx, 2, 2 * td, slots), BF16),
            pltpu.VMEM((nx, 2, 2 * td, 128), F32),
            pltpu.VMEM((nx, slots, feats), BF16),
            pltpu.VMEM((2, 2, nz, 2, slots, feats), BF16),
            pltpu.VMEM((2, feats, 3 * hid), BF16),
            pltpu.VMEM((2, nz, slots, 3 * hid), F32),
            exchange,
            exchange,
            pltpu.VMEM((2, nz, 2, slots, 3 * hid), BF16),
            pltpu.VMEM((2, nz, 2, slots, feats), F32),
            outs,
            outs,
            ring_slots,
            ring_slots,
            ring_slots,
            ring_slots,
            pltpu.VMEM((2, 2, slots, feats), BF16),
            pltpu.VMEM((nx, slots, feats), BF16),
            pltpu.VMEM((2, nq, 2 * td, feats // nq), BF16),
            pltpu.VMEM((nyl, 2 * td, feats // nq), BF16),
            pltpu.VMEM((3, 2 * feats, hid), BF16),
            pltpu.SemaphoreType.DMA((SEMAPHORES,)),
            pltpu.SemaphoreType.DMA((SEMAPHORES,)),
            pltpu.SemaphoreType.DMA((9,)),
        ],
        compiler_params=pltpu.CompilerParams(
            collective_id=0, has_side_effects=True, vmem_limit_bytes=60 * 1024 * 1024
        ),
        name="moe_layer",
    )(tokens, grad_out, expert_ids.T, gate_probs.T, gate_weight, up_weight, down_weight)
    return pl.pallas_call(
        hand_on,
        out_shape=tuple(jax.ShapeDtypeStruct(one.shape, one.dtype) for one in results),
        in_specs=[vmem] * 5,
        out_specs=(vmem,) * 5,
        name="hand_on",
    )(*results)


def hand_on(*refs):
    for source, target in zip(refs[:5], refs[5:]):
        target[...] = source[...]


def solution(mesh):
    return jax.shard_map(
        functools.partial(local, mesh.shape["section"] // 2),
        mesh=mesh,
        in_specs=(
            P(("expert", "dp"), None),
            P(("expert", "dp"), None),
            P(("expert", "dp"), None),
            P(("expert", "dp"), None),
            P("dp", ("expert", "section")),
            P("dp", ("expert", "section")),
            P("dp", ("expert", "section")),
        ),
        out_specs=(
            P(("expert", "dp"), "section"),
            P(("expert", "dp"), "section"),
            P("dp", ("expert", "section")),
            P("dp", ("expert", "section")),
            P("dp", ("expert", "section")),
        ),
        check_vma=False,
    )
```

time: 406 us -> 103 us (0.25)
  waiting for transfers between devices: 188 us -> 0 us
  blocking collectives: 136 us -> 0 us
  Pallas kernels: 0 us -> 102 us
  local copies, waits for them, and re-layouts: 25 us -> 0 us
  matrix products: 20.4 us -> 0 us
  starting transfers between devices: 13.8 us -> 0 us
  between operations: 13.9 us -> 0.64 us
  other arithmetic: 5.84 us -> 0 us
    all_gather x5 -> x0, blocking collectives: 136 us -> none  [the longest x1 40.5 us: local(): lax.all_gather(expert_ids.astype(jnp.float32), 'expert', axis=0, tiled=True)]
    all_to_all x2 -> x0, waiting for transfers between devices: 125 us -> none  [the longest x1 65.2 us: local(): lax.all_to_all(partial_in.reshape(expert_devices, capacity, model_width)....]
    pallas_call x0 -> x2, Pallas kernels: none -> 102 us  [the longest x1 100 us: local(): pl.pallas_call(functools.partial(kernel, (nx, nz, nyl, feats, hid, td)),...]
    unnamed x7 -> x0, waiting for transfers between devices: 32.8 us -> none
    all_gather x2 -> x0, waiting for transfers between devices: 30.1 us -> none  [the longest x1 30.1 us: local(): lax.all_gather(grad_out, 'expert', axis=0, tiled=True)]
    dot_general x13 -> x0, matrix products: 20.4 us -> none  [the longest x1 4.63 us: local(): jnp.einsum('pct,ptd->pcd', pick_bf, src_scaled, preferred_element_type=jn...]
    all_to_all x2 -> x0, starting transfers between devices: 13.4 us -> none  [the longest x1 7.34 us: local(): lax.all_to_all(partial_in.reshape(expert_devices, capacity, model_width)....]
    unnamed x19 -> x0, local copies, waits for them, and re-layouts: 10 us -> none
  transfers between devices with their start and end apart: 7 -> 0, of which waited for: 4 -> 0; matrix products, arithmetic and copies ran while one was open for 8% -> 0% of each run, Pallas kernels for 0% -> 0%
where the time goes in v2:
time: 103 us
  Pallas kernels  102 us (99%)
    pallas_call x1, Pallas kernels, local(): pl.pallas_call(functools.partial(kernel, (nx, nz, nyl, feats, hid, td)),...  100 us
    pallas_call x1, Pallas kernels, local(): pl.pallas_call(hand_on, out_shape=tuple((jax.ShapeDtypeStruct(one.shape,...  2.31 us

profile of v2, /device:TPU:1, one launch (start us, length us, event | category | flops | bytes accessed | tf_op | source)
XLA Modules:
  0.0 103.1 jit_solution(12221019693918654624)
XLA Ops:
  0.6 100.2 %moe_layer.1 = (bf16[16,384]{1,0:T(8,128)(2,1)}, bf16[16,384]{1,0:T(8,128)(2,1)}, bf16[1536,128]{1,0:T(8,128)(2,1)}, bf16[1536,128]{1,0:T(8,128)(2,1)}, bf16[1536,128]{1,0:T(8,128)(2,1)}) custom-call(bf16[16,3072]{1,0:T(8,128)(2,1)} %tok.1, bf16[16,3072]{1,0:T(8,128)(2,1)} %grd.1, s32[2,16]{1,0:T(2,128)} %bitcast.2, f32[2,16]{1,0:T(2,128)} %bitcast.3, ...), custom_call_target="tpu_custom_call" | custom-call | tf_op jit(solution)/shard_map/moe_layer/pallas_call | solution.py:425
  100.8 2.3 %hand_on.1 = (bf16[16,384]{1,0:T(8,128)(2,1)}, bf16[16,384]{1,0:T(8,128)(2,1)}, bf16[1536,128]{1,0:T(8,128)(2,1)}, bf16[1536,128]{1,0:T(8,128)(2,1)}, bf16[1536,128]{1,0:T(8,128)(2,1)}) custom-call(bf16[16,384]{1,0:T(8,128)(2,1)} %get-tuple-element.10.refs_0_, bf16[16,384]{1,0:T(8,128)(2,1)} %get-tuple-element.11.refs_1_, ...), custom_call_target="tpu_custom_call" | custom-call | tf_op jit(solution)/shard_map/hand_on/pallas_call | solution.py:464

commit v3 on v2

--- a/solution.py
+++ b/solution.py
@@ -161,12 +161,15 @@
     def columns_of(ref, i):
         return ref.at[:, pl.ds(i * width, width)]
 
-    def gather_send(t, k, p):
+    def gather_start(j):
+        t, p = j // 2, j % 2
         for i in range(2):
+            part = columns_of(gathered.at[c, t, 0, p], i)
+            if j:
+                arrived(("expert", j, i), part)
             for side, to in ((0, above), (1, below)):
-                if sends(t, k, p, side):
-                    part = columns_of(gathered.at[c, t, 0, p], i)
-                    go(("gather", t, k, p, i, side), part, columns_of(gathered.at[c, t, landing(k, side), p], i), to)
+                if sends(t, 1, p, side):
+                    go(("gather", t, 1, p, i, side), part, columns_of(gathered.at[c, t, landing(1, side), p], i), to)
 
     def gather_take(t, k):
         for p in range(2):
@@ -289,14 +292,20 @@
         lax.fori_loop(first, last, turn, 0)
 
     gathered[c, 0, 0, 0] = pick_for(x)
-    gather_send(0, 1, 0)
-    for j in range(1, nx):
+    gather_start(0)
+    for j in sorted(range(1, nx), key=lambda j: min(j, nx - j)):
         e = ring(x + j, nx)
         rsend[j] = pick_for(e)
-        go(("expert", j), rsend.at[j], gathered.at[c, j // 2, 0, j % 2], at(e, z, y, c))
-    arrived(("expert", 1), gathered.at[c, 0, 0, 1])
-    gather_send(0, 1, 1)
+        for i in range(2):
+            part = columns_of(gathered.at[c, j // 2, 0, j % 2], i)
+            go(("expert", j, i), columns_of(rsend.at[j], i), part, at(e, z, y, c))
+    gather_start(1)
     twin_share(0, 0)
+
+    def enter():
+        for j in (3, 2):
+            gather_start(j)
+        twin_share(1, 0)
 
     def valid(k):
         return 0 <= k <= half
@@ -305,49 +314,49 @@
         if turn <= half:
             gather_take(0, turn)
         if turn == LAG:
-            for p in range(2):
-                arrived(("expert", 2 + p), gathered.at[c, 1, 0, p])
-                gather_send(1, 1, p)
-            twin_share(1, 0)
+            enter()
         if turn == 1:
             for load in loads:
                 load.wait()
-        if valid(turn - 1):
+        if turn <= half:
             compute_h(0, turn - 1)
         if turn > LAG:
             gather_take(1, turn - LAG)
         if valid(turn - LAG - 1):
             compute_h(1, turn - LAG - 1)
-        if valid(turn - 3):
+        if turn == half:
+            compute_h(0, half)
+        if valid(turn - 3) and turn < half + LAG:
             outputs(0, turn - 3)
-        if valid(turn - LAG - 3):
-            outputs(1, turn - LAG - 3)
     compute_h(1, half)
-    for k in range(half + LAG - 2, half + 1):
+    outputs(0, half)
+    for k in range(half + LAG - 3, half):
         outputs(0, k)
     sum_step(0, 1)
-    for step in range(2, half):
-        outputs(1, half + step - 4)
+    outputs(1, 0)
+    if half > 2:
+        sum_step(0, 2)
+    for k in range(1, half + 1):
+        outputs(1, k)
+    for step in range(3, half):
         sum_step(0, step)
-    for k in range(2 * half - 4, half + 1):
-        outputs(1, k)
     sum_step(1, 1)
     weight_grads(0, tiles // 6)
     sum_step(0, half)
-    weight_grads(tiles // 6, tiles // 3)
     sum_step(1, 2)
-    weight_grads(tiles // 3, tiles // 2)
+    weight_grads(tiles // 6, tiles // 2)
     sum_end(0)
     for step in range(3, half):
         sum_step(1, step)
-    weight_grads(tiles // 2, tiles)
+    weight_grads(tiles // 2, 5 * tiles // 6)
+    if half > 2:
+        sum_step(1, half)
+    weight_grads(5 * tiles // 6, tiles)
     results = []
     for i, ref in enumerate((d_gate, d_up, d_down)):
         result = pltpu.make_async_copy(grads.at[i], ref, load_sem.at[6 + i])
         result.start()
         results.append(result)
-    if half > 2:
-        sum_step(1, half)
     combined = combine(0)
     sum_end(1)
     combined = (combined + combine(1)).astype(BF16)

time: 103 us -> 101 us (0.981)
  Pallas kernels: 102 us -> 100 us
    pallas_call x1, Pallas kernels: 100 us -> 98.2 us  [local(): pl.pallas_call(functools.partial(kernel, (nx, nz, nyl, feats, hid, td)),...]
where the time goes in v3:
time: 101 us
  Pallas kernels  100 us (99%)
    pallas_call x1, Pallas kernels, local(): pl.pallas_call(functools.partial(kernel, (nx, nz, nyl, feats, hid, td)),...  98.2 us
    pallas_call x1, Pallas kernels, local(): pl.pallas_call(hand_on, out_shape=tuple((jax.ShapeDtypeStruct(one.shape,...  2.31 us

profile of v3, /device:TPU:1, one launch (start us, length us, event | category | flops | bytes accessed | tf_op | source)
XLA Modules:
  0.0 101.1 jit_solution(4788972978951052329)
XLA Ops:
  0.6 98.2 %moe_layer.1 = (bf16[16,384]{1,0:T(8,128)(2,1)}, bf16[16,384]{1,0:T(8,128)(2,1)}, bf16[1536,128]{1,0:T(8,128)(2,1)}, bf16[1536,128]{1,0:T(8,128)(2,1)}, bf16[1536,128]{1,0:T(8,128)(2,1)}) custom-call(bf16[16,3072]{1,0:T(8,128)(2,1)} %tok.1, bf16[16,3072]{1,0:T(8,128)(2,1)} %grd.1, s32[2,16]{1,0:T(2,128)} %bitcast.2, f32[2,16]{1,0:T(2,128)} %bitcast.3, ...), custom_call_target="tpu_custom_call" | custom-call | tf_op jit(solution)/shard_map/moe_layer/pallas_call | solution.py:434
  98.8 2.3 %hand_on.1 = (bf16[16,384]{1,0:T(8,128)(2,1)}, bf16[16,384]{1,0:T(8,128)(2,1)}, bf16[1536,128]{1,0:T(8,128)(2,1)}, bf16[1536,128]{1,0:T(8,128)(2,1)}, bf16[1536,128]{1,0:T(8,128)(2,1)}) custom-call(bf16[16,384]{1,0:T(8,128)(2,1)} %get-tuple-element.10.refs_0_, bf16[16,384]{1,0:T(8,128)(2,1)} %get-tuple-element.11.refs_1_, ...), custom_call_target="tpu_custom_call" | custom-call | tf_op jit(solution)/shard_map/hand_on/pallas_call | solution.py:473

commit v4 on v3

--- a/solution.py
+++ b/solution.py
@@ -473,15 +473,24 @@
     return pl.pallas_call(
         hand_on,
         out_shape=tuple(jax.ShapeDtypeStruct(one.shape, one.dtype) for one in results),
-        in_specs=[vmem] * 5,
-        out_specs=(vmem,) * 5,
+        in_specs=[anywhere] * 5,
+        out_specs=(anywhere,) * 5,
+        scratch_shapes=[pltpu.VMEM(one.shape, one.dtype) for one in results] + [pltpu.SemaphoreType.DMA((10,))],
         name="hand_on",
     )(*results)
 
 
 def hand_on(*refs):
-    for source, target in zip(refs[:5], refs[5:]):
-        target[...] = source[...]
+    sem = refs[15]
+    taken = [pltpu.make_async_copy(refs[i], refs[10 + i], sem.at[i]) for i in range(5)]
+    given = [pltpu.make_async_copy(refs[10 + i], refs[5 + i], sem.at[5 + i]) for i in range(5)]
+    for one in taken:
+        one.start()
+    for one, other in zip(taken, given):
+        one.wait()
+        other.start()
+    for other in given:
+        other.wait()
 
 
 def solution(mesh):

time: 101 us -> 101 us (level)
  no operation moved by 1% of the time
where the time goes in v4:
time: 101 us
  Pallas kernels  100 us (99%)
    pallas_call x1, Pallas kernels, local(): pl.pallas_call(functools.partial(kernel, (nx, nz, nyl, feats, hid, td)),...  98.2 us
    pallas_call x1, Pallas kernels, local(): pl.pallas_call(hand_on, out_shape=tuple((jax.ShapeDtypeStruct(one.shape,...  2.12 us

profile of v4, /device:TPU:1, one launch (start us, length us, event | category | flops | bytes accessed | tf_op | source)
XLA Modules:
  0.0 100.9 jit_solution(2082561060174084374)
XLA Ops:
  0.6 98.2 %moe_layer.1 = (bf16[16,384]{1,0:T(8,128)(2,1)}, bf16[16,384]{1,0:T(8,128)(2,1)}, bf16[1536,128]{1,0:T(8,128)(2,1)}, bf16[1536,128]{1,0:T(8,128)(2,1)}, bf16[1536,128]{1,0:T(8,128)(2,1)}) custom-call(bf16[16,3072]{1,0:T(8,128)(2,1)} %tok.1, bf16[16,3072]{1,0:T(8,128)(2,1)} %grd.1, s32[2,16]{1,0:T(2,128)} %bitcast.2, f32[2,16]{1,0:T(2,128)} %bitcast.3, ...), custom_call_target="tpu_custom_call" | custom-call | tf_op jit(solution)/shard_map/moe_layer/pallas_call | solution.py:434
  98.8 2.1 %hand_on.1 = (bf16[16,384]{1,0:T(8,128)(2,1)}, bf16[16,384]{1,0:T(8,128)(2,1)}, bf16[1536,128]{1,0:T(8,128)(2,1)}, bf16[1536,128]{1,0:T(8,128)(2,1)}, bf16[1536,128]{1,0:T(8,128)(2,1)}) custom-call(bf16[16,384]{1,0:T(8,128)(2,1)} %get-tuple-element.10.refs_0_, bf16[16,384]{1,0:T(8,128)(2,1)} %get-tuple-element.11.refs_1_, ...), custom_call_target="tpu_custom_call" | custom-call | tf_op jit(solution)/shard_map/hand_on/pallas_call | solution.py:473
